TPU v7x, 32 devices: a whole 2x2x4 slice. The times are simulated.
32 devices in a mesh: groups: 2 (over y), tile: 4 (over z), pair: 2 (over x), sub: 2 (over core).
Axes of the slice: x: 2, y: 2, z: 4, core: 2. Of those that a mesh axis runs over, the one named last changes fastest.
Arguments:
- ref_chips: bfloat16 [4, 256, 4096], P(('groups', 'pair'), ('tile', 'sub')), parts along dimension 0, may hold values from -300 to 700
- search_windows: bfloat16 [4, 512, 16384], P(('groups', 'pair'), ('tile', 'sub')), parts along dimension 0, may hold values from -300 to 700
- dest_block: int32 [4, 512, 1], P(('groups', 'pair'), ('tile', 'sub')), parts along dimension 0, may hold values from 0 to 7; in each aligned block of 64 rows (0 to 63, 64 to 127, ..., all dimensions but the last counted through in order) at most 16 rows name the same one
- dest_slot: int32 [4, 512], P(('groups', 'pair'), ('tile', 'sub')), parts along dimension 0, may hold values from 0 to 31
Outputs:
- smoothed_scores: float32 [4, 256, 4096], P(('groups', 'pair'), ('tile', 'sub')), parts along dimension 0
There are 2 independent parts, one for each index of `groups`. A program takes and returns all parts, laid end to end along the dimension named above; each array names one. Nothing has to cross between parts.
Inputs may be any that keep to these rules, and one draw needn't show every extreme that they name: `dest_block`: in the rows of one device (aligned blocks of 64 windows), no block index is named by more than 16 windows.
All inputs are finite; a program needn't handle non-finite values.
Results may differ from a plain program's by a relative error of at most 0.0003.
Values may be sent and summed in bfloat16 or wider, within the bound.
No kernel may reach another device: no remote copies, remote signals or barrier semaphores. Data moves between devices by JAX's collectives and lax.ppermute only.
A program may use at most 64 MiB of HBM per device.

v0:
```python
import math
import jax
import jax.numpy as jnp
from jax import lax
from jax.sharding import PartitionSpec as P

CHIP = 64
WIN = 128
GC = 8
precise = lax.Precision.HIGHEST
epsilon = 1e-06


def padded(block, sides, width):
    for axis, dim in sides:
        count = lax.axis_size(axis)
        forward = [(i, i + 1) for i in range(count - 1)]
        backward = [(target, source) for source, target in forward]
        low = lax.ppermute(
            lax.slice_in_dim(block, block.shape[dim] - width, None, axis=dim), axis, forward
        )
        high = lax.ppermute(lax.slice_in_dim(block, 0, width, axis=dim), axis, backward)
        block = jnp.concatenate([low, block, high], axis=dim)
    return block


def tables(length, width):
    freqs = jnp.arange(length, dtype=jnp.int32)[:, None]
    places = jnp.arange(width, dtype=jnp.int32)[None, :]
    phase = freqs * places % length
    angle = phase.astype(jnp.float32) * (2.0 * math.pi / length)
    return (jnp.cos(angle), jnp.sin(angle))


def spectrum(image, cosine, sine_table):
    first_real = jnp.einsum("kn,bnm->bkm", cosine, image, precision=precise)
    first_imag = -jnp.einsum("kn,bnm->bkm", sine_table, image, precision=precise)
    spec_real = jnp.einsum("bkm,lm->bkl", first_real, cosine, precision=precise) + jnp.einsum(
        "bkm,lm->bkl", first_imag, sine_table, precision=precise
    )
    spec_imag = jnp.einsum("bkm,lm->bkl", first_imag, cosine, precision=precise) - jnp.einsum(
        "bkm,lm->bkl", first_real, sine_table, precision=precise
    )
    return (spec_real, spec_imag)


def centre(chips_raw, chip_side):
    chip_float = chips_raw.astype(jnp.float32).reshape(-1, chip_side, chip_side)
    centred = chip_float - jnp.mean(chip_float, axis=(1, 2), keepdims=True)
    chip_std = jnp.sqrt(jnp.mean(centred * centred, axis=(1, 2)) + epsilon)
    return (centred, chip_std)


def match(chip_real, chip_imag, chip_std, windows_raw, chip_side, window_side):
    offsets = window_side - chip_side
    cos_full, sin_full = tables(window_side, window_side)
    cos_part = cos_full[:offsets]
    sin_part = sin_full[:offsets]
    window_float = windows_raw.astype(jnp.float32).reshape(-1, window_side, window_side)
    win_real, win_imag = spectrum(window_float, cos_full, sin_full)
    product_real = chip_real * win_real + chip_imag * win_imag
    product_imag = chip_real * win_imag - chip_imag * win_real
    half_real = jnp.einsum("ak,bkl->bal", cos_part, product_real, precision=precise) - jnp.einsum(
        "ak,bkl->bal", sin_part, product_imag, precision=precise
    )
    half_imag = jnp.einsum("ak,bkl->bal", cos_part, product_imag, precision=precise) + jnp.einsum(
        "ak,bkl->bal", sin_part, product_real, precision=precise
    )
    numerator = (
        jnp.einsum("bal,el->bae", half_real, cos_part, precision=precise)
        - jnp.einsum("bal,el->bae", half_imag, sin_part, precision=precise)
    ) / (window_side * window_side)
    starts = jnp.arange(offsets, dtype=jnp.int32)[:, None]
    pixels = jnp.arange(window_side, dtype=jnp.int32)[None, :]
    window_band = ((pixels >= starts) & (pixels < starts + chip_side)).astype(jnp.float32)
    first_rows = jnp.einsum("ax,bxy->bay", window_band, window_float, precision=precise)
    first_sum = jnp.einsum("bay,ey->bae", first_rows, window_band, precision=precise)
    second_rows = jnp.einsum(
        "ax,bxy->bay", window_band, window_float * window_float, precision=precise
    )
    second_sum = jnp.einsum("bay,ey->bae", second_rows, window_band, precision=precise)
    patch_mean = first_sum / (chip_side * chip_side)
    patch_var = second_sum / (chip_side * chip_side) - patch_mean * patch_mean
    score = numerator / (chip_side * chip_std[:, None, None] * jnp.sqrt(patch_var + epsilon))
    return score.reshape(-1, offsets * offsets)


def in_blocks(function, operands):
    amount = operands[0].shape[0]
    block_rows = 16
    shaped = tuple(
        (item.reshape((amount // block_rows, block_rows) + item.shape[1:]) for item in operands)
    )
    result = lax.map(lambda grouped: function(*grouped), shaped)
    return result.reshape(amount, -1)


def on_device(ref_chips, search_windows, dest_block, dest_slot):
    chips = ref_chips[0]
    windows = search_windows[0]
    targets = dest_block[0, :, 0]
    target_slot = dest_slot[0]
    chip_side = CHIP
    window_side = WIN
    offsets = window_side - chip_side
    window_amount = windows.shape[0]
    chip_amount = chips.shape[0]
    devices = lax.axis_size(("tile", "sub"))
    capacity = max(2, 2 * window_amount // devices)
    slot_amount = devices * capacity
    order = jnp.arange(window_amount, dtype=jnp.int32)
    matches = targets[:, None] == targets[None, :]
    earlier = order[:, None] > order[None, :]
    ranking = jnp.sum((matches & earlier).astype(jnp.int32), axis=1)
    positions = targets * capacity + ranking
    slot_buffer = jnp.full((slot_amount,), -1, jnp.int32).at[positions].set(target_slot)
    cos_chip, sin_chip = tables(window_side, chip_side)
    requests = slot_buffer.reshape(devices, capacity)
    found = jnp.take(
        chips,
        jnp.maximum(
            lax.all_to_all(requests, ("tile", "sub"), split_axis=0, concat_axis=0, tiled=True), 0
        ),
        axis=0,
    )
    fetched = lax.all_to_all(found, ("tile", "sub"), split_axis=0, concat_axis=0, tiled=True)
    own_chips = jnp.take(fetched.reshape(slot_amount, chip_side * chip_side), positions, axis=0)

    def match_own(chip_part, window_part):
        centred_part, std_part = centre(chip_part, chip_side)
        real_part, imag_part = spectrum(centred_part, cos_chip, sin_chip)
        return match(real_part, imag_part, std_part, window_part, chip_side, window_side)

    own_scores = in_blocks(match_own, (own_chips, windows))
    score_buffer = (
        jnp.zeros((slot_amount, offsets * offsets), jnp.float32).at[positions].set(own_scores)
    )
    scores, slots_here = (
        lax.all_to_all(score_buffer, ("tile", "sub"), split_axis=0, concat_axis=0, tiled=True),
        lax.all_to_all(slot_buffer, ("tile", "sub"), split_axis=0, concat_axis=0, tiled=True),
    )
    hits_table = (slots_here[None, :] == jnp.arange(chip_amount, dtype=jnp.int32)[:, None]).astype(
        jnp.float32
    )
    total = jnp.dot(hits_table, scores, precision=precise)
    looks = jnp.sum(hits_table, axis=1)
    average = total / jnp.maximum(looks, 1.0)[:, None]
    grid = average.reshape(-1, GC, offsets * offsets)
    extended = padded(grid, ((("tile", "sub"), 0),), 1)
    vertical = extended[:-2] + extended[2:]
    sideways = jnp.pad(grid, ((0, 0), (1, 1), (0, 0)))
    horizontal = sideways[:, :-2] + sideways[:, 2:]
    smoothed = (4.0 * grid + vertical + horizontal) / 8.0
    return smoothed.reshape(1, chip_amount, offsets * offsets)


def solution(mesh):
    return jax.shard_map(
        on_device,
        mesh=mesh,
        in_specs=(
            P(("groups", "pair"), ("tile", "sub"), None),
            P(("groups", "pair"), ("tile", "sub"), None),
            P(("groups", "pair"), ("tile", "sub"), None),
            P(("groups", "pair"), ("tile", "sub")),
        ),
        out_specs=P(("groups", "pair"), ("tile", "sub"), None),
        check_vma=False,
    )
```

profile of v0, /device:TPU:1, one launch (start us, length us, event | category | flops | bytes accessed | tf_op | source)
XLA Modules:
  0.0 226.2 jit_solution(14719844709658617581)
XLA Ops:
  2.6 11.0 %all_to_all.35 = s32[8,1,16]{2,1,0:T(1,128)S(1)} all-to-all(s32[8,1,16]{2,1,0:T(1,128)S(1)} %bitcast.236), channel_id=1, replica_groups=mesh['groups'=2,'tile'=4,'pair'=2,'sub'=2] {'tile','sub'}, dimensions={0} | all-to-all | bytes 1024 | tf_op jit(solution)/shard_map/all_to_all | solution.py:122
  16.1 4.2 %all-to-all-start.2 = ((bf16[8,16,4096]{2,1,0:T(8,128)(2,1)}), bf16[8,16,4096]{2,1,0:T(8,128)(2,1)S(1)}, u32[]{:S(2)}, u32[]{:S(2)}) async-start(bf16[8,16,4096]{2,1,0:T(8,128)(2,1)} %broadcast_select_fusion), calls=%async_computation.2 | async-start | bytes 2097152 | tf_op jit(solution)/shard_map/all_to_all | solution.py:126
  21.1 24.7 %all-to-all-done.2 = bf16[8,16,4096]{2,1,0:T(8,128)(2,1)S(1)} async-done(((bf16[8,16,4096]{2,1,0:T(8,128)(2,1)}), bf16[8,16,4096]{2,1,0:T(8,128)(2,1)S(1)}, u32[]{:S(2)}, u32[]{:S(2)}) %all-to-all-start.2) | async-done | bytes 1048608 | tf_op jit(solution)/shard_map/all_to_all | solution.py:126
  45.9 4.2 %all-to-all-start = ((s32[8,16,1]{1,2,0:T(1,128)}), s32[8,16,1]{1,2,0:T(1,128)S(1)}, u32[]{:S(2)}, u32[]{:S(2)}) async-start(s32[8,16,1]{1,2,0:T(1,128)} %bitcast.5), calls=%async_computation | async-start | bytes 8192 | tf_op jit(solution)/shard_map/all_to_all | solution.py:140
  51.0 109.2 %while.14 = (s32[]{:T(128)}, f32[4,16,4096]{2,1,0:T(8,128)S(1)}, bf16[4,16,4096]{2,1,0:T(8,128)(2,1)S(1)}, bf16[4,16,16384]{2,1,0:T(8,128)(2,1)}, s32[]{:T(128)}) while((s32[]{:T(128)}, f32[4,16,4096]{2,1,0:T(8,128)S(1)}, bf16[4,16,4096]{2,1,0:T(8,128)(2,1)S(1)}, bf16[4,16,16384]{2,1,0:T(8,128)(2,1)}, s32[]{:T(128)}) %tuple.39), condition=%wide.region_5.6_spmd.clone.clone, body=%wide.region_2.5_spmd.clone.clone.sunk | while | flops 4872994816 | bytes 46598104 | solution.py:94
  58.1 2.0 fusion.248
  60.1 1.9 convolution_add_fusion.5
  62.1 1.9 fusion.252
  64.0 1.9 convolution_subtract_fusion.5
  71.5 1.9 multiply_subtract_fusion.2
  85.4 2.0 fusion.248
  87.4 1.9 convolution_add_fusion.5
  89.3 1.9 fusion.252
  91.3 1.9 convolution_subtract_fusion.5
  98.7 1.9 multiply_subtract_fusion.2
  112.7 2.0 fusion.248
  114.6 1.9 convolution_add_fusion.5
  116.6 1.9 fusion.252
  118.5 1.9 convolution_subtract_fusion.5
  122.3 1.8 convolution_add_fusion.6
  126.0 1.9 multiply_subtract_fusion.2
  139.9 2.0 fusion.248
  141.9 1.9 convolution_add_fusion.5
  143.8 1.9 fusion.252
  145.8 1.9 convolution_subtract_fusion.5
  153.2 1.9 multiply_subtract_fusion.2
  160.3 2.6 %scatter_custom_fusion.1 = f32[128,4096]{1,0:T(8,128)} fusion(s32[64]{0:T(128)S(1)} %fusion.136, f32[64,4096]{1,0:T(8,128)S(1)} %bitcast.237, f32[]{:T(128)} %constant.141.clone.1), kind=kCustom, calls=%fused_computation.150 | custom fusion | bytes 2097156 | tf_op jit(solution)/shard_map/scatter | solution.py:136
  162.9 5.1 %all-to-all-start.3 = ((f32[8,16,4096]{2,1,0:T(8,128)}), f32[8,16,4096]{2,1,0:T(8,128)S(1)}, u32[]{:S(2)}, u32[]{:S(2)}) async-start(f32[8,16,4096]{2,1,0:T(8,128)} %bitcast.15), calls=%async_computation.3 | async-start | bytes 4194304 | tf_op jit(solution)/shard_map/all_to_all | solution.py:139
  169.4 46.7 %all-to-all-done.3 = f32[8,16,4096]{2,1,0:T(8,128)S(1)} async-done(((f32[8,16,4096]{2,1,0:T(8,128)}), f32[8,16,4096]{2,1,0:T(8,128)S(1)}, u32[]{:S(2)}, u32[]{:S(2)}) %all-to-all-start.3) | async-done | bytes 2097184 | tf_op jit(solution)/shard_map/all_to_all | solution.py:139
  217.0 1.9 collective-permute-start
  218.9 2.4 %collective-permute-start.1 = (f32[1,8,4096]{2,1,0:T(8,128)S(1)}, f32[1,8,4096]{2,1,0:T(8,128)S(1)}, u32[]{:S(2)}, u32[]{:S(2)}) collective-permute-start(f32[1,8,4096]{2,1,0:T(8,128)S(1)} %get-tuple-element.139), channel_id=1, source_target_pairs={{1,0},{4,1},{5,4},{8,5},{9,8},{12,9},{13,12},{3,2},{6,3},{7,6},{10... | collective-permute-start | bytes 393224 | tf_op jit(solution)/shard_map/ppermute | solution.py:22
  221.3 3.9 %collective-permute-done.1 = f32[1,8,4096]{2,1,0:T(8,128)S(1)} collective-permute-done((f32[1,8,4096]{2,1,0:T(8,128)S(1)}, f32[1,8,4096]{2,1,0:T(8,128)S(1)}, u32[]{:S(2)}, u32[]{:S(2)}) %collective-permute-start.1) | collective-permute-done | bytes 131104 | tf_op jit(solution)/shard_map/ppermute | solution.py:22
  (156 shorter events, 77.5 us)
Async XLA Ops:
  0.0 13.7 %copy-start = (bf16[1,32,4096]{2,1,0:T(8,128)(2,1)S(1)}, bf16[1,32,4096]{2,1,0:T(8,128)(2,1)}, u32[]{:S(2)}) copy-start(bf16[1,32,4096]{2,1,0:T(8,128)(2,1)} %param.6) | copy-start | bytes 786436
  14.9 6.1 %copy-start.1 = (s32[1,64,1]{1,2,0:T(1,128)S(1)}, s32[1,64,1]{1,2,0:T(1,128)}, u32[]{:S(2)}) copy-start(s32[1,64,1]{1,2,0:T(1,128)} %param.8) | copy-start | bytes 772
  16.1 29.8 %all-to-all-start.2 = ((bf16[8,16,4096]{2,1,0:T(8,128)(2,1)}), bf16[8,16,4096]{2,1,0:T(8,128)(2,1)S(1)}, u32[]{:S(2)}, u32[]{:S(2)}) async-start(bf16[8,16,4096]{2,1,0:T(8,128)(2,1)} %broadcast_select_fusion), calls=%async_computation.2 | async-start | bytes 2097152 | tf_op jit(solution)/shard_map/all_to_all | solution.py:126
  45.9 117.0 %all-to-all-start = ((s32[8,16,1]{1,2,0:T(1,128)}), s32[8,16,1]{1,2,0:T(1,128)S(1)}, u32[]{:S(2)}, u32[]{:S(2)}) async-start(s32[8,16,1]{1,2,0:T(1,128)} %bitcast.5), calls=%async_computation | async-start | bytes 8192 | tf_op jit(solution)/shard_map/all_to_all | solution.py:140
  162.9 53.2 %all-to-all-start.3 = ((f32[8,16,4096]{2,1,0:T(8,128)}), f32[8,16,4096]{2,1,0:T(8,128)S(1)}, u32[]{:S(2)}, u32[]{:S(2)}) async-start(f32[8,16,4096]{2,1,0:T(8,128)} %bitcast.15), calls=%async_computation.3 | async-start | bytes 4194304 | tf_op jit(solution)/shard_map/all_to_all | solution.py:139
  217.0 4.3 %collective-permute-start = (f32[1,8,4096]{2,1,0:T(8,128)S(1)}, f32[1,8,4096]{2,1,0:T(8,128)S(1)}, u32[]{:S(2)}, u32[]{:S(2)}) collective-permute-start(f32[1,8,4096]{2,1,0:T(8,128)S(1)} %get-tuple-element.138), channel_id=1, source_target_pairs={{0,1},{1,4},{4,5},{5,8},{8,9},{9,12},{12,13},{2,3},{3,6},{6,7},{7,... | collective-permute-start | bytes 393224 | tf_op jit(solution)/shard_map/ppermute | solution.py:19
  218.9 6.3 %collective-permute-start.1 = (f32[1,8,4096]{2,1,0:T(8,128)S(1)}, f32[1,8,4096]{2,1,0:T(8,128)S(1)}, u32[]{:S(2)}, u32[]{:S(2)}) collective-permute-start(f32[1,8,4096]{2,1,0:T(8,128)S(1)} %get-tuple-element.139), channel_id=1, source_target_pairs={{1,0},{4,1},{5,4},{8,5},{9,8},{12,9},{13,12},{3,2},{6,3},{7,6},{10... | collective-permute-start | bytes 393224 | tf_op jit(solution)/shard_map/ppermute | solution.py:22
where the time goes:
time: 227 us; the launch traced here: 226 us
  matrix products  98 us (43%)
  waiting for transfers between devices  75.3 us (33%)
  starting transfers between devices  17.8 us (8%)
  local copies, waits for them, and re-layouts  14.4 us (6%)
  blocking collectives  11 us (5%)
  other arithmetic  8.43 us (4%)
    all_to_all x1, waiting for transfers between devices, on_device(): lax.all_to_all(score_buffer, ('tile', 'sub'), split_axis=0, concat_axis=0...  46.7 us
    all_to_all x1, waiting for transfers between devices, on_device(): lax.all_to_all(found, ('tile', 'sub'), split_axis=0, concat_axis=0, tiled...  24.7 us
    dot_general x8, matrix products, spectrum(): jnp.einsum('bkm,lm->bkl', first_real, sine_table, precision=precise)  15.5 us
    dot_general x8, matrix products, spectrum(): jnp.einsum('bkm,lm->bkl', first_real, cosine, precision=precise)  15.1 us
    dot_general x8, matrix products, spectrum(): jnp.einsum('bkm,lm->bkl', first_imag, sine_table, precision=precise)  15.1 us
    dot_general x8, matrix products, spectrum(): jnp.einsum('bkm,lm->bkl', first_imag, cosine, precision=precise)  15 us
    all_to_all x1, blocking collectives, on_device(): lax.all_to_all(requests, ('tile', 'sub'), split_axis=0, concat_axis=0, ti...  11 us
    dot_general x8, matrix products, spectrum(): first_real = jnp.einsum('kn,bnm->bkm', cosine, image, precision=precise)  6.31 us
  transfers between devices with their start and end apart: 5, of which 3 were waited for; matrix products, arithmetic and copies ran while one was open for 50% of the time, Pallas kernels for 0%

commit v1 on v0

--- a/solution.py
+++ b/solution.py
@@ -9,6 +9,22 @@
 GC = 8
 precise = lax.Precision.HIGHEST
 epsilon = 1e-06
+
+
+def swapped_with_each(x, axis, split, join):
+    ways, here = (lax.axis_size(axis), lax.axis_index(axis))
+    width = x.shape[split] // ways
+    lengths = list(x.shape)
+    lengths[split] = width
+    height = lengths[join]
+    lengths[join] = height * ways
+    full = jnp.zeros(lengths, x.dtype)
+    for mask in range(ways):
+        part = lax.dynamic_slice_in_dim(x, (here ^ mask) * width, width, axis=split)
+        if mask:
+            part = lax.ppermute(part, axis, [(d, d ^ mask) for d in range(ways)])
+        full = lax.dynamic_update_slice_in_dim(full, part, (here ^ mask) * height, axis=join)
+    return full
 
 
 def padded(block, sides, width):
@@ -123,7 +139,7 @@
         ),
         axis=0,
     )
-    fetched = lax.all_to_all(found, ("tile", "sub"), split_axis=0, concat_axis=0, tiled=True)
+    fetched = swapped_with_each(found, ("tile", "sub"), 0, 0)
     own_chips = jnp.take(fetched.reshape(slot_amount, chip_side * chip_side), positions, axis=0)
 
     def match_own(chip_part, window_part):

time: 227 us -> 225 us (level)
  starting transfers between devices: 17.8 us -> 29.3 us
  blocking collectives: 11 us -> 0 us
  waiting for transfers between devices: 75.3 us -> 72.1 us
    all_to_all x1, waiting for transfers between devices: 24.7 us -> 3.3 us  [on_device(): lax.all_to_all(requests, ('tile', 'sub'), split_axis=0, concat_axis=0, ti...]
    ppermute x0 -> x7, waiting for transfers between devices: none -> 18.2 us  [swapped_with_each(): part = lax.ppermute(part, axis, [(d, d ^ mask) for d in range(ways)])]
    all_to_all x1 -> x0, blocking collectives: 11 us -> none  [on_device(): lax.all_to_all(requests, ('tile', 'sub'), split_axis=0, concat_axis=0, ti...]
    ppermute x0 -> x7, starting transfers between devices: none -> 10.9 us  [swapped_with_each(): part = lax.ppermute(part, axis, [(d, d ^ mask) for d in range(ways)])]
  transfers between devices with their start and end apart: 5 -> 12, of which waited for: 3 -> 5; matrix products, arithmetic and copies ran while one was open for 50% -> 52% of each run, Pallas kernels for 0% -> 0%
where the time goes in v1:
time: 225 us; the launch traced here: 224 us
  matrix products  98 us (44%)
  waiting for transfers between devices  72.1 us (32%)
  starting transfers between devices  29.3 us (13%)
  local copies, waits for them, and re-layouts  15.2 us (7%)
  other arithmetic  8.09 us (4%)
    all_to_all x1, waiting for transfers between devices, on_device(): lax.all_to_all(score_buffer, ('tile', 'sub'), split_axis=0, concat_axis=0...  46.7 us
    ppermute x7, waiting for transfers between devices, swapped_with_each(): part = lax.ppermute(part, axis, [(d, d ^ mask) for d in range(ways)])  18.2 us
    dot_general x8, matrix products, spectrum(): jnp.einsum('bkm,lm->bkl', first_real, sine_table, precision=precise)  15.5 us
    dot_general x8, matrix products, spectrum(): jnp.einsum('bkm,lm->bkl', first_real, cosine, precision=precise)  15.1 us
    dot_general x8, matrix products, spectrum(): jnp.einsum('bkm,lm->bkl', first_imag, sine_table, precision=precise)  15.1 us
    dot_general x8, matrix products, spectrum(): jnp.einsum('bkm,lm->bkl', first_imag, cosine, precision=precise)  15 us
    ppermute x7, starting transfers between devices, swapped_with_each(): part = lax.ppermute(part, axis, [(d, d ^ mask) for d in range(ways)])  10.9 us
    all_to_all x1, starting transfers between devices, on_device(): lax.all_to_all(requests, ('tile', 'sub'), split_axis=0, concat_axis=0, ti...  6.37 us
  transfers between devices with their start and end apart: 12, of which 5 were waited for; matrix products, arithmetic and copies ran while one was open for 52% of the time, Pallas kernels for 0%

profile of v1, /device:TPU:1, one launch (start us, length us, event | category | flops | bytes accessed | tf_op | source)
XLA Modules:
  0.0 224.3 jit_solution(10990145025154354654)
XLA Ops:
  3.2 6.4 %all-to-all-start.1 = ((s32[8,1,16]{2,1,0:T(1,128)}), s32[8,1,16]{2,1,0:T(1,128)S(1)}, u32[]{:S(2)}, u32[]{:S(2)}) async-start(s32[8,1,16]{2,1,0:T(1,128)} %bitcast.6), calls=%async_computation.1 | async-start | bytes 8192 | tf_op jit(solution)/shard_map/all_to_all | solution.py:138
  11.0 3.3 %all-to-all-done.1 = s32[8,1,16]{2,1,0:T(1,128)S(1)} async-done(((s32[8,1,16]{2,1,0:T(1,128)}), s32[8,1,16]{2,1,0:T(1,128)S(1)}, u32[]{:S(2)}, u32[]{:S(2)}) %all-to-all-start.1) | async-done | bytes 544 | tf_op jit(solution)/shard_map/all_to_all | solution.py:138
  14.3 3.9 %all-to-all-start = ((s32[8,16,1]{1,2,0:T(1,128)}), s32[8,16,1]{1,2,0:T(1,128)S(1)}, u32[]{:S(2)}, u32[]{:S(2)}) async-start(s32[8,16,1]{1,2,0:T(1,128)} %bitcast.5), calls=%async_computation | async-start | bytes 8192 | tf_op jit(solution)/shard_map/all_to_all | solution.py:156
  20.1 3.5 %collective-permute-start.6 = (bf16[1,16,4096]{2,1,0:T(8,128)(2,1)S(1)}, bf16[1,16,4096]{2,1,0:T(8,128)(2,1)S(1)}, u32[]{:S(2)}, u32[]{:S(2)}) collective-permute-start(bf16[1,16,4096]{2,1,0:T(8,128)(2,1)S(1)} %get-tuple-element.138), channel_id=1, source_target_pairs={{0,13},{1,12},{4,9},{5,8},{8,5},{9,4},{12,1},{13,0},{2,15},{3,14},... | collective-permute-start | bytes 393224 | tf_op jit(solution)/shard_map/ppermute | solution.py:25
  27.8 9.9 %collective-permute-done.1 = bf16[1,16,4096]{2,1,0:T(8,128)(2,1)S(1)} collective-permute-done((bf16[1,16,4096]{2,1,0:T(8,128)(2,1)S(1)}, bf16[1,16,4096]{2,1,0:T(8,128)(2,1)S(1)}, u32[]{:S(2)}, u32[]{:S(2)}) %collective-permute-start.1) | collective-permute-done | bytes 131104 | tf_op jit(solution)/shard_map/ppermute | solution.py:25
  37.7 3.1 %collective-permute-start.2 = (bf16[1,16,4096]{2,1,0:T(8,128)(2,1)S(1)}, bf16[1,16,4096]{2,1,0:T(8,128)(2,1)S(1)}, u32[]{:S(2)}, u32[]{:S(2)}) collective-permute-start(bf16[1,16,4096]{2,1,0:T(8,128)(2,1)S(1)} %get-tuple-element.142), channel_id=1, source_target_pairs={{0,5},{1,4},{4,1},{5,0},{8,13},{9,12},{12,9},{13,8},{2,7},{3,6},{6... | collective-permute-start | bytes 393224 | tf_op jit(solution)/shard_map/ppermute | solution.py:25
  40.7 8.3 %collective-permute-done.2 = bf16[1,16,4096]{2,1,0:T(8,128)(2,1)S(1)} collective-permute-done((bf16[1,16,4096]{2,1,0:T(8,128)(2,1)S(1)}, bf16[1,16,4096]{2,1,0:T(8,128)(2,1)S(1)}, u32[]{:S(2)}, u32[]{:S(2)}) %collective-permute-start.2) | collective-permute-done | bytes 131104 | tf_op jit(solution)/shard_map/ppermute | solution.py:25
  50.2 109.4 %while.14 = (s32[]{:T(128)}, f32[4,16,4096]{2,1,0:T(8,128)S(1)}, bf16[4,16,4096]{2,1,0:T(8,128)(2,1)S(1)}, bf16[4,16,16384]{2,1,0:T(8,128)(2,1)}, s32[]{:T(128)}) while((s32[]{:T(128)}, f32[4,16,4096]{2,1,0:T(8,128)S(1)}, bf16[4,16,4096]{2,1,0:T(8,128)(2,1)S(1)}, bf16[4,16,16384]{2,1,0:T(8,128)(2,1)}, s32[]{:T(128)}) %tuple.46), condition=%wide.region_5.6_spmd.clone.clone, body=%wide.region_2.5_spmd.clone.clone.sunk | while | flops 4872994816 | bytes 46598104 | solution.py:110
  57.4 2.0 fusion.248
  59.4 1.9 convolution_add_fusion.5
  61.4 1.9 fusion.252
  63.3 1.9 convolution_subtract_fusion.5
  70.8 1.9 multiply_subtract_fusion.2
  84.7 2.0 fusion.248
  86.7 1.9 convolution_add_fusion.5
  88.6 1.9 fusion.252
  90.6 1.9 convolution_subtract_fusion.5
  112.0 2.0 fusion.248
  113.9 1.9 convolution_add_fusion.5
  115.9 1.9 fusion.252
  117.8 1.9 convolution_subtract_fusion.5
  125.3 1.9 multiply_subtract_fusion.2
  139.2 2.0 fusion.248
  141.2 1.9 convolution_add_fusion.5
  143.1 1.9 fusion.252
  145.1 1.9 convolution_subtract_fusion.5
  152.5 1.9 multiply_subtract_fusion.2
  159.6 2.6 %scatter_custom_fusion.1 = f32[128,4096]{1,0:T(8,128)} fusion(s32[64]{0:T(128)S(1)} %fusion.136, f32[64,4096]{1,0:T(8,128)S(1)} %bitcast.236, f32[]{:T(128)} %constant.156.clone.1), kind=kCustom, calls=%fused_computation.150 | custom fusion | bytes 2097156 | tf_op jit(solution)/shard_map/scatter | solution.py:152
  162.2 3.9 %all-to-all-start.2 = ((f32[8,16,4096]{2,1,0:T(8,128)}), f32[8,16,4096]{2,1,0:T(8,128)S(1)}, u32[]{:S(2)}, u32[]{:S(2)}) async-start(f32[8,16,4096]{2,1,0:T(8,128)} %bitcast.15), calls=%async_computation.2 | async-start | bytes 4194304 | tf_op jit(solution)/shard_map/all_to_all | solution.py:155
  167.5 46.7 %all-to-all-done.2 = f32[8,16,4096]{2,1,0:T(8,128)S(1)} async-done(((f32[8,16,4096]{2,1,0:T(8,128)}), f32[8,16,4096]{2,1,0:T(8,128)S(1)}, u32[]{:S(2)}, u32[]{:S(2)}) %all-to-all-start.2) | async-done | bytes 2097184 | tf_op jit(solution)/shard_map/all_to_all | solution.py:155
  217.0 2.4 %collective-permute-start.8 = (f32[1,8,4096]{2,1,0:T(8,128)S(1)}, f32[1,8,4096]{2,1,0:T(8,128)S(1)}, u32[]{:S(2)}, u32[]{:S(2)}) collective-permute-start(f32[1,8,4096]{2,1,0:T(8,128)S(1)} %get-tuple-element.147), channel_id=1, source_target_pairs={{1,0},{4,1},{5,4},{8,5},{9,8},{12,9},{13,12},{3,2},{6,3},{7,6},{10... | collective-permute-start | bytes 393224 | tf_op jit(solution)/shard_map/ppermute | solution.py:38
  219.5 3.9 %collective-permute-done.8 = f32[1,8,4096]{2,1,0:T(8,128)S(1)} collective-permute-done((f32[1,8,4096]{2,1,0:T(8,128)S(1)}, f32[1,8,4096]{2,1,0:T(8,128)S(1)}, u32[]{:S(2)}, u32[]{:S(2)}) %collective-permute-start.8) | collective-permute-done | bytes 131104 | tf_op jit(solution)/shard_map/ppermute | solution.py:38
  (176 shorter events, 88.0 us)
Async XLA Ops:
  0.0 18.3 %copy-start = (bf16[1,32,4096]{2,1,0:T(8,128)(2,1)S(1)}, bf16[1,32,4096]{2,1,0:T(8,128)(2,1)}, u32[]{:S(2)}) copy-start(bf16[1,32,4096]{2,1,0:T(8,128)(2,1)} %param.6) | copy-start | bytes 786436
  3.2 11.2 %all-to-all-start.1 = ((s32[8,1,16]{2,1,0:T(1,128)}), s32[8,1,16]{2,1,0:T(1,128)S(1)}, u32[]{:S(2)}, u32[]{:S(2)}) async-start(s32[8,1,16]{2,1,0:T(1,128)} %bitcast.6), calls=%async_computation.1 | async-start | bytes 8192 | tf_op jit(solution)/shard_map/all_to_all | solution.py:138
  14.3 147.9 %all-to-all-start = ((s32[8,16,1]{1,2,0:T(1,128)}), s32[8,16,1]{1,2,0:T(1,128)S(1)}, u32[]{:S(2)}, u32[]{:S(2)}) async-start(s32[8,16,1]{1,2,0:T(1,128)} %bitcast.5), calls=%async_computation | async-start | bytes 8192 | tf_op jit(solution)/shard_map/all_to_all | solution.py:156
  19.9 6.5 %collective-permute-start = (bf16[1,16,4096]{2,1,0:T(8,128)(2,1)S(1)}, bf16[1,16,4096]{2,1,0:T(8,128)(2,1)S(1)}, u32[]{:S(2)}, u32[]{:S(2)}) collective-permute-start(bf16[1,16,4096]{2,1,0:T(8,128)(2,1)S(1)} %get-tuple-element.144), channel_id=1, source_target_pairs={{0,1},{1,0},{4,5},{5,4},{8,9},{9,8},{12,13},{13,12},{2,3},{3,2},{6... | collective-permute-start | bytes 393224 | tf_op jit(solution)/shard_map/ppermute | solution.py:25
  20.1 29.0 %collective-permute-start.6 = (bf16[1,16,4096]{2,1,0:T(8,128)(2,1)S(1)}, bf16[1,16,4096]{2,1,0:T(8,128)(2,1)S(1)}, u32[]{:S(2)}, u32[]{:S(2)}) collective-permute-start(bf16[1,16,4096]{2,1,0:T(8,128)(2,1)S(1)} %get-tuple-element.138), channel_id=1, source_target_pairs={{0,13},{1,12},{4,9},{5,8},{8,5},{9,4},{12,1},{13,0},{2,15},{3,14},... | collective-permute-start | bytes 393224 | tf_op jit(solution)/shard_map/ppermute | solution.py:25
  23.6 25.5 %collective-permute-start.5 = (bf16[1,16,4096]{2,1,0:T(8,128)(2,1)S(1)}, bf16[1,16,4096]{2,1,0:T(8,128)(2,1)S(1)}, u32[]{:S(2)}, u32[]{:S(2)}) collective-permute-start(bf16[1,16,4096]{2,1,0:T(8,128)(2,1)S(1)} %get-tuple-element.139), channel_id=1, source_target_pairs={{0,12},{1,13},{4,8},{5,9},{8,4},{9,5},{12,0},{13,1},{2,14},{3,15},... | collective-permute-start | bytes 393224 | tf_op jit(solution)/shard_map/ppermute | solution.py:25
  23.7 25.3 %collective-permute-start.4 = (bf16[1,16,4096]{2,1,0:T(8,128)(2,1)S(1)}, bf16[1,16,4096]{2,1,0:T(8,128)(2,1)S(1)}, u32[]{:S(2)}, u32[]{:S(2)}) collective-permute-start(bf16[1,16,4096]{2,1,0:T(8,128)(2,1)S(1)} %get-tuple-element.140), channel_id=1, source_target_pairs={{0,9},{1,8},{4,13},{5,12},{8,1},{9,0},{12,5},{13,4},{2,11},{3,10},... | collective-permute-start | bytes 393224 | tf_op jit(solution)/shard_map/ppermute | solution.py:25
  24.8 24.3 %collective-permute-start.3 = (bf16[1,16,4096]{2,1,0:T(8,128)(2,1)S(1)}, bf16[1,16,4096]{2,1,0:T(8,128)(2,1)S(1)}, u32[]{:S(2)}, u32[]{:S(2)}) collective-permute-start(bf16[1,16,4096]{2,1,0:T(8,128)(2,1)S(1)} %get-tuple-element.141), channel_id=1, source_target_pairs={{0,8},{1,9},{4,12},{5,13},{8,0},{9,1},{12,4},{13,5},{2,10},{3,11},... | collective-permute-start | bytes 393224 | tf_op jit(solution)/shard_map/ppermute | solution.py:25
  26.4 11.3 %collective-permute-start.1 = (bf16[1,16,4096]{2,1,0:T(8,128)(2,1)S(1)}, bf16[1,16,4096]{2,1,0:T(8,128)(2,1)S(1)}, u32[]{:S(2)}, u32[]{:S(2)}) collective-permute-start(bf16[1,16,4096]{2,1,0:T(8,128)(2,1)S(1)} %get-tuple-element.143), channel_id=1, source_target_pairs={{0,4},{1,5},{4,0},{5,1},{8,12},{9,13},{12,8},{13,9},{2,6},{3,7},{6... | collective-permute-start | bytes 393224 | tf_op jit(solution)/shard_map/ppermute | solution.py:25
  37.7 11.3 %collective-permute-start.2 = (bf16[1,16,4096]{2,1,0:T(8,128)(2,1)S(1)}, bf16[1,16,4096]{2,1,0:T(8,128)(2,1)S(1)}, u32[]{:S(2)}, u32[]{:S(2)}) collective-permute-start(bf16[1,16,4096]{2,1,0:T(8,128)(2,1)S(1)} %get-tuple-element.142), channel_id=1, source_target_pairs={{0,5},{1,4},{4,1},{5,0},{8,13},{9,12},{12,9},{13,8},{2,7},{3,6},{6... | collective-permute-start | bytes 393224 | tf_op jit(solution)/shard_map/ppermute | solution.py:25
  162.2 52.0 %all-to-all-start.2 = ((f32[8,16,4096]{2,1,0:T(8,128)}), f32[8,16,4096]{2,1,0:T(8,128)S(1)}, u32[]{:S(2)}, u32[]{:S(2)}) async-start(f32[8,16,4096]{2,1,0:T(8,128)} %bitcast.15), calls=%async_computation.2 | async-start | bytes 4194304 | tf_op jit(solution)/shard_map/all_to_all | solution.py:155
  215.1 4.3 %collective-permute-start.7 = (f32[1,8,4096]{2,1,0:T(8,128)S(1)}, f32[1,8,4096]{2,1,0:T(8,128)S(1)}, u32[]{:S(2)}, u32[]{:S(2)}) collective-permute-start(f32[1,8,4096]{2,1,0:T(8,128)S(1)} %get-tuple-element.146), channel_id=1, source_target_pairs={{0,1},{1,4},{4,5},{5,8},{8,9},{9,12},{12,13},{2,3},{3,6},{6,7},{7,... | collective-permute-start | bytes 393224 | tf_op jit(solution)/shard_map/ppermute | solution.py:35
  217.0 6.3 %collective-permute-start.8 = (f32[1,8,4096]{2,1,0:T(8,128)S(1)}, f32[1,8,4096]{2,1,0:T(8,128)S(1)}, u32[]{:S(2)}, u32[]{:S(2)}) collective-permute-start(f32[1,8,4096]{2,1,0:T(8,128)S(1)} %get-tuple-element.147), channel_id=1, source_target_pairs={{1,0},{4,1},{5,4},{8,5},{9,8},{12,9},{13,12},{3,2},{6,3},{7,6},{10... | collective-permute-start | bytes 393224 | tf_op jit(solution)/shard_map/ppermute | solution.py:38
